TPU v7x, 256 devices: a whole 4x4x8 slice. The times are simulated.
256 devices in a mesh: gx: 32 (over z, y_hi, core), gy: 8 (over y_lo, x).
Axes of the slice: x: 4, y: 4 (y_hi: 2, y_lo: 2; y = y_hi * 2 + y_lo), z: 8, core: 2. Of those that a mesh axis runs over, the one named last changes fastest.
Arguments:
- velocity: float32 [256, 256, 256], P('gx', 'gy'), may hold values from 1.5 to 4.5
- density: float32 [256, 256, 256], P('gx', 'gy'), may hold values from 1.8 to 2.6
- adjoint_last: float32 [256, 256, 256], P('gx', 'gy'), may hold values from -6 to 6
- adjoint_now: float32 [256, 256, 256], P('gx', 'gy'), may hold values from -6 to 6
- forward_accel: bfloat16 [8, 256, 256, 256], P(None, 'gx', 'gy'), may hold values from -6 to 6
- residual_panels: bfloat16 [131072, 128], P(('gx', 'gy')), may hold values from -6 to 6
- owner_slab: int32 [131072, 1], P(('gx', 'gy')), may hold values from 0 to 31; in each aligned block of 512 rows (0 to 511, 512 to 1023, ...) at most 32 rows name the same one
- receiver_cell: int32 [131072], P(('gx', 'gy')), may hold values from 0 to 65535
- trace_offset: int32 [131072], P(('gx', 'gy')), may hold values from 0 to 31
Outputs:
- sensitivity: float32 [128, 128, 128], P('gx', 'gy')
- adjoint_final: float32 [256, 256, 256], P('gx', 'gy')
Inputs may be any that keep to these rules, and one draw needn't show every extreme that they name: `owner_slab`: the rows of one device name one slab at most 32 times, a bound that some block reaches. `receiver_cell`: numbered (x * 32 + y) * 256 + z within the owner's block.
All inputs are finite; a program needn't handle non-finite values.
Results may differ from a plain program's by a relative error of at most 0.0003.
Values may be sent and summed in bfloat16 or wider, within the bound.
A program may use at most 64 MiB of HBM per device.

v0:
```python
import jax
import jax.numpy as jnp
from jax import lax
from jax.sharding import PartitionSpec as P


def padded_2(array, sides, width):
    for axis, dim in sides:
        devices, length = (lax.axis_size(axis), array.shape[dim])
        up = [(i, (i + 1) % devices) for i in range(devices - 1)]
        down = [(j, i) for i, j in up]
        last = lax.slice_in_dim(array, length - width, length, axis=dim)
        leading = lax.slice_in_dim(array, 0, width, axis=dim)
        before = lax.ppermute(last, axis, up)
        after = lax.ppermute(leading, axis, down)
        array = jnp.concatenate([before, array, after], axis=dim)
    return array


def resample(panels, offsets, step_count):
    panel_len = panels.shape[1]
    half_width = panel_len // step_count
    values = panels.astype(jnp.float32)
    clock = (jnp.arange(panel_len, dtype=jnp.int32)[None, :] + offsets[:, None]).astype(jnp.float32)
    columns = []
    for moment in range(step_count):
        weights = (
            jnp.maximum(0.0, 1.0 - jnp.abs(clock - half_width * (moment + 1)) / half_width) * 0.25
        )
        columns.append(jnp.sum(values * weights, axis=1))
    return jnp.stack(columns, axis=1)


def face_list(padded):
    return [
        padded[2:, 1:-1, 1:-1],
        padded[:-2, 1:-1, 1:-1],
        padded[1:-1, 2:, 1:-1],
        padded[1:-1, :-2, 1:-1],
        padded[1:-1, 1:-1, 2:],
        padded[1:-1, 1:-1, :-2],
    ]


def coarsen(kernel):
    size_a, size_b, size_c = kernel.shape
    blocks = kernel.reshape(size_a // 2, 2, size_b // 2, 2, size_c // 2, 2)
    return jnp.sum(blocks, axis=(1, 3, 5)) * 0.125


def wave_step(wave, wave_prev, couplings):
    padded = padded_2(wave, (("gx", 0), ("gy", 1)), 1)
    padded = jnp.pad(padded, ((0, 0), (0, 0), (1, 1)))
    nearby = face_list(padded)
    laplace = couplings[0] * (nearby[0] - wave)
    for index in range(1, 6):
        laplace = laplace + couplings[index] * (nearby[index] - wave)
    return 2.0 * wave - wave_prev + laplace


def shards(
    velocity,
    density,
    adjoint_last,
    adjoint_now,
    forward_accel,
    residual_panels,
    owner_slab,
    receiver_cell,
    trace_offset,
):
    slab_count = lax.axis_size("gx")
    sensors = residual_panels.shape[0]
    slot_count = sensors // 16
    step_count = forward_accel.shape[0]
    panel_len = residual_panels.shape[1]
    shift_span = 2 * panel_len // step_count
    owners = owner_slab[:, 0]
    onehot = (owners[:, None] == jnp.arange(slab_count, dtype=jnp.int32)[None, :]).astype(jnp.int32)
    order_rank = jnp.sum(jnp.cumsum(onehot, axis=0) * onehot, axis=1) - 1
    target = owners * slot_count + order_rank
    packed = (
        jnp.zeros((slab_count * slot_count, panel_len), jnp.bfloat16)
        .at[target]
        .set(residual_panels)
    )
    codes = (
        jnp.zeros((slab_count * slot_count,), jnp.int32)
        .at[target]
        .set(receiver_cell * shift_span + trace_offset)
    )
    arrived, arrived_codes = (
        lax.all_to_all(
            packed.reshape(slab_count, slot_count, panel_len),
            "gx",
            split_axis=0,
            concat_axis=0,
            tiled=True,
        ),
        lax.all_to_all(
            codes.reshape(slab_count, slot_count), "gx", split_axis=0, concat_axis=0, tiled=True
        ),
    )
    arrived_codes = arrived_codes.reshape(-1)
    cell_ids = arrived_codes // shift_span
    amplitudes = resample(arrived.reshape(-1, panel_len), arrived_codes % shift_span, step_count)
    square = 0.11 * velocity
    stiffness = square * square * density
    rho_pad = padded_2(density, (("gx", 0), ("gy", 1)), 1)
    rho_pad = jnp.pad(rho_pad, ((0, 0), (0, 0), (1, 1)))
    couplings = [stiffness * (2.0 / (density + nearby)) for nearby in face_list(rho_pad)]
    wave_prev = adjoint_last
    wave = adjoint_now
    accumulated = jnp.zeros(wave.shape, jnp.float32)
    for moment in range(step_count):
        wave_next = wave_step(wave, wave_prev, couplings)
        wave_next = (
            wave_next.reshape(-1).at[cell_ids].add(amplitudes[:, moment]).reshape(wave.shape)
        )
        accumulated = accumulated + wave_next * forward_accel[moment].astype(jnp.float32)
        wave_prev, wave = (wave, wave_next)
    kernel = -2.0 / velocity * accumulated
    coarse_block = jnp.transpose(coarsen(kernel), (0, 2, 1))
    sensitivity = lax.all_to_all(coarse_block, "gy", split_axis=1, concat_axis=2, tiled=True)
    return (sensitivity, wave)


def solution(mesh):
    in_specs = (
        P("gx", "gy", None),
        P("gx", "gy", None),
        P("gx", "gy", None),
        P("gx", "gy", None),
        P(None, "gx", "gy", None),
        P(("gx", "gy"), None),
        P(("gx", "gy"), None),
        P(("gx", "gy")),
        P(("gx", "gy")),
    )
    out_specs = (P("gx", "gy", None), P("gx", "gy", None))
    return jax.shard_map(shards, mesh=mesh, in_specs=in_specs, out_specs=out_specs, check_vma=False)
```

profile of v0, /device:TPU:113, one launch (start us, length us, event | category | flops | bytes accessed | tf_op | source)
XLA Modules:
  0.0 328.7 jit_solution(6253343978235181013)
XLA Ops:
  15.9 10.6 %all-to-all-start = ((s32[32,1,32]{2,1,0:T(1,128)}), s32[32,1,32]{2,1,0:T(1,128)S(1)}, u32[]{:S(2)}, u32[]{:S(2)}) async-start(s32[32,1,32]{2,1,0:T(1,128)} %all_to_all.22), calls=%async_computation | async-start | bytes 32768 | tf_op jit(solution)/shard_map/all_to_all | solution.py:100
  36.6 10.3 %all-to-all-start.1 = ((bf16[32,32,128]{2,1,0:T(8,128)(2,1)}), bf16[32,32,128]{2,1,0:T(8,128)(2,1)S(1)}, u32[]{:S(2)}, u32[]{:S(2)}) async-start(bf16[32,32,128]{2,1,0:T(8,128)(2,1)} %bitcast.6), calls=%async_computation.1 | async-start | bytes 524288 | tf_op jit(solution)/shard_map/all_to_all | solution.py:93
  66.4 6.2 %scatter_fusion = f32[65536]{0:T(1024)S(1)} fusion(f32[65536]{0:T(1024)S(1)} %bitcast.73, s32[1024]{0:T(1024)S(1)} %bitcast.92, f32[1024]{0:T(1024)S(1)} %reshape.458), kind=kCustom, calls=%fused_computation.2 | custom fusion | flops 1024 | bytes 16384 | tf_op jit(solution)/shard_map/scatter-add | solution.py:118
  72.6 7.2 %collective-permute-start.9 = (f32[1,32,256]{2,1,0:T(8,128)S(1)}, f32[1,32,256]{2,1,0:T(8,128)S(1)}, u32[]{:S(2)}, u32[]{:S(2)}) collective-permute-start(f32[1,32,256]{2,1,0:T(8,128)S(1)} %slice.571), channel_id=1, source_target_pairs={{0,8},{8,16},{16,24},{24,32},{32,40},{40,48},{48,56},{56,64},{64,7... | collective-permute-start | bytes 98312 | tf_op jit(solution)/shard_map/ppermute | solution.py:14
  81.9 6.9 %collective-permute-done.8 = f32[1,32,256]{2,1,0:T(8,128)S(1)} collective-permute-done((f32[1,32,256]{2,1,0:T(8,128)S(1)}, f32[1,32,256]{2,1,0:T(8,128)S(1)}, u32[]{:S(2)}, u32[]{:S(2)}) %collective-permute-start.8) | collective-permute-done | bytes 32800 | tf_op jit(solution)/shard_map/ppermute | solution.py:15
  96.2 6.2 %scatter_fusion.1 = f32[65536]{0:T(1024)S(1)} fusion(f32[65536]{0:T(1024)S(1)} %bitcast.74, s32[1024]{0:T(1024)S(1)} %bitcast.93, f32[1024]{0:T(1024)S(1)} %reshape.466), kind=kCustom, calls=%fused_computation.3 | custom fusion | flops 1024 | bytes 16384 | tf_op jit(solution)/shard_map/scatter-add | solution.py:118
  108.1 6.9 %collective-permute-done.12 = f32[1,32,256]{2,1,0:T(8,128)S(1)} collective-permute-done((f32[1,32,256]{2,1,0:T(8,128)S(1)}, f32[1,32,256]{2,1,0:T(8,128)S(1)}, u32[]{:S(2)}, u32[]{:S(2)}) %collective-permute-start.12) | collective-permute-done | bytes 32800 | tf_op jit(solution)/shard_map/ppermute | solution.py:15
  122.4 6.2 %scatter_fusion.2 = f32[65536]{0:T(1024)S(1)} fusion(f32[65536]{0:T(1024)S(1)} %bitcast.75, s32[1024]{0:T(1024)S(1)} %bitcast.94, f32[1024]{0:T(1024)S(1)} %reshape.474), kind=kCustom, calls=%fused_computation.4 | custom fusion | flops 1024 | bytes 16384 | tf_op jit(solution)/shard_map/scatter-add | solution.py:118
  134.4 6.9 %collective-permute-done.16 = f32[1,32,256]{2,1,0:T(8,128)S(1)} collective-permute-done((f32[1,32,256]{2,1,0:T(8,128)S(1)}, f32[1,32,256]{2,1,0:T(8,128)S(1)}, u32[]{:S(2)}, u32[]{:S(2)}) %collective-permute-start.16) | collective-permute-done | bytes 32800 | tf_op jit(solution)/shard_map/ppermute | solution.py:15
  150.3 6.2 %scatter_fusion.3 = f32[65536]{0:T(1024)S(1)} fusion(f32[65536]{0:T(1024)S(1)} %bitcast.76, s32[1024]{0:T(1024)S(1)} %bitcast.95, f32[1024]{0:T(1024)S(1)} %reshape.482), kind=kCustom, calls=%fused_computation.5 | custom fusion | flops 1024 | bytes 16384 | tf_op jit(solution)/shard_map/scatter-add | solution.py:118
  162.2 6.9 %collective-permute-done.20 = f32[1,32,256]{2,1,0:T(8,128)S(1)} collective-permute-done((f32[1,32,256]{2,1,0:T(8,128)S(1)}, f32[1,32,256]{2,1,0:T(8,128)S(1)}, u32[]{:S(2)}, u32[]{:S(2)}) %collective-permute-start.20) | collective-permute-done | bytes 32800 | tf_op jit(solution)/shard_map/ppermute | solution.py:15
  170.4 6.6 %collective-permute-start.23 = (f32[10,1,256]{2,1,0:T(1,128)S(1)}, f32[10,1,256]{2,1,0:T(1,128)S(1)}, u32[]{:S(2)}, u32[]{:S(2)}) collective-permute-start(f32[10,1,256]{2,1,0:T(1,128)S(1)} %get-tuple-element.23), channel_id=1, source_target_pairs={{0,1},{1,2},{2,3},{3,4},{4,5},{5,6},{6,7},{8,9},{9,10},{10,11},{11... | collective-permute-start | bytes 30728 | tf_op jit(solution)/shard_map/ppermute | solution.py:14
  178.7 6.2 %scatter_fusion.4 = f32[65536]{0:T(1024)S(1)} fusion(f32[65536]{0:T(1024)S(1)} %bitcast.77, s32[1024]{0:T(1024)S(1)} %bitcast.96, f32[1024]{0:T(1024)S(1)} %reshape.490), kind=kCustom, calls=%fused_computation.6 | custom fusion | flops 1024 | bytes 16384 | tf_op jit(solution)/shard_map/scatter-add | solution.py:118
  190.6 6.9 %collective-permute-done.24 = f32[1,32,256]{2,1,0:T(8,128)S(1)} collective-permute-done((f32[1,32,256]{2,1,0:T(8,128)S(1)}, f32[1,32,256]{2,1,0:T(8,128)S(1)}, u32[]{:S(2)}, u32[]{:S(2)}) %collective-permute-start.24) | collective-permute-done | bytes 32800 | tf_op jit(solution)/shard_map/ppermute | solution.py:15
  198.8 6.6 %collective-permute-start.27 = (f32[10,1,256]{2,1,0:T(1,128)S(1)}, f32[10,1,256]{2,1,0:T(1,128)S(1)}, u32[]{:S(2)}, u32[]{:S(2)}) collective-permute-start(f32[10,1,256]{2,1,0:T(1,128)S(1)} %get-tuple-element.21), channel_id=1, source_target_pairs={{0,1},{1,2},{2,3},{3,4},{4,5},{5,6},{6,7},{8,9},{9,10},{10,11},{11... | collective-permute-start | bytes 30728 | tf_op jit(solution)/shard_map/ppermute | solution.py:14
  207.1 6.2 %scatter_fusion.5 = f32[65536]{0:T(1024)S(1)} fusion(f32[65536]{0:T(1024)S(1)} %bitcast.78, s32[1024]{0:T(1024)S(1)} %bitcast.97, f32[1024]{0:T(1024)S(1)} %reshape.498), kind=kCustom, calls=%fused_computation.7 | custom fusion | flops 1024 | bytes 16384 | tf_op jit(solution)/shard_map/scatter-add | solution.py:118
  220.2 7.1 %collective-permute-done.28 = f32[1,32,256]{2,1,0:T(8,128)S(1)} collective-permute-done((f32[1,32,256]{2,1,0:T(8,128)}, f32[1,32,256]{2,1,0:T(8,128)S(1)}, u32[]{:S(2)}, u32[]{:S(2)}) %collective-permute-start.28) | collective-permute-done | bytes 32800 | tf_op jit(solution)/shard_map/ppermute | solution.py:15
  229.2 7.2 %collective-permute-start.31 = (f32[10,1,256]{2,1,0:T(1,128)}, f32[10,1,256]{2,1,0:T(1,128)}, u32[]{:S(2)}, u32[]{:S(2)}) collective-permute-start(f32[10,1,256]{2,1,0:T(1,128)} %get-tuple-element.19), channel_id=1, source_target_pairs={{0,1},{1,2},{2,3},{3,4},{4,5},{5,6},{6,7},{8,9},{9,10},{10,11},{11... | collective-permute-start | bytes 30728 | tf_op jit(solution)/shard_map/ppermute | solution.py:14
  240.0 6.3 %scatter_fusion.6 = f32[65536]{0:T(1024)S(1)} fusion(f32[65536]{0:T(1024)S(1)} %bitcast.79, s32[1024]{0:T(1024)S(1)} %bitcast.98, f32[1024]{0:T(1024)} %reshape.506), kind=kCustom, calls=%fused_computation.8 | custom fusion | flops 1024 | bytes 16384 | tf_op jit(solution)/shard_map/scatter-add | solution.py:118
  262.5 6.8 %collective-permute-start.35 = (f32[10,1,256]{2,1,0:T(1,128)}, f32[10,1,256]{2,1,0:T(1,128)}, u32[]{:S(2)}, u32[]{:S(2)}) collective-permute-start(f32[10,1,256]{2,1,0:T(1,128)} %get-tuple-element.17), channel_id=1, source_target_pairs={{0,1},{1,2},{2,3},{3,4},{4,5},{5,6},{6,7},{8,9},{9,10},{10,11},{11... | collective-permute-start | bytes 30728 | tf_op jit(solution)/shard_map/ppermute | solution.py:14
  273.4 6.3 %scatter_fusion.7 = f32[65536]{0:T(1024)S(1)} fusion(f32[65536]{0:T(1024)S(1)} %bitcast.80, s32[1024]{0:T(1024)S(1)} %bitcast.99, f32[1024]{0:T(1024)} %reshape.514), kind=kCustom, calls=%fused_computation.9 | custom fusion | flops 1024 | bytes 16384 | tf_op jit(solution)/shard_map/scatter-add | solution.py:118
  281.7 18.1 %reshape.429 = f32[4,2,16,2,128,2]{5,4,3,2,1,0:T(8,128)} reshape(f32[8,32,256]{2,1,0:T(8,128)S(1)} %fusion.154) | data formatting | bytes 524288 | tf_op jit(solution)/shard_map/reshape | solution.py:47
  299.8 7.0 %reduce_sum.123 = f32[4,16,128]{2,1,0:T(8,128)S(1)} reduce(f32[4,2,16,2,128,2]{5,4,3,2,1,0:T(8,128)} %reshape.429, f32[]{:T(128)} %constant.71.clone.1), dimensions={1,3,5}, to_apply=%region_21.22 | reduce | flops 57344 | bytes 294916 | tf_op jit(solution)/shard_map/reduce_sum | solution.py:48
  307.2 19.1 %all_to_all.32 = f32[8,1,1024]{2,1,0:T(1,128)S(1)} all-to-all(f32[8,1,1024]{2,1,0:T(1,128)S(1)} %reshape.532), channel_id=1, replica_groups=mesh['gx'=32,'gy'=8] {'gy'}, dimensions={0} | all-to-all | bytes 65536 | tf_op jit(solution)/shard_map/all_to_all | solution.py:124
  (194 shorter events, 136.1 us)
Async XLA Ops:
  1.5 46.8 %collective-permute-start.2 = (f32[1,32,256]{2,1,0:T(8,128)S(1)}, f32[1,32,256]{2,1,0:T(8,128)S(1)}, u32[]{:S(2)}, u32[]{:S(2)}) collective-permute-start(f32[1,32,256]{2,1,0:T(8,128)S(1)} %get-tuple-element.49), channel_id=1, source_target_pairs={{0,8},{8,16},{16,24},{24,32},{32,40},{40,48},{48,56},{56,64},{64,7... | collective-permute-start | bytes 98312 | tf_op jit(solution)/shard_map/ppermute | solution.py:14
  6.6 42.7 %collective-permute-start = (f32[1,32,256]{2,1,0:T(8,128)S(1)}, f32[1,32,256]{2,1,0:T(8,128)S(1)}, u32[]{:S(2)}, u32[]{:S(2)}) collective-permute-start(f32[1,32,256]{2,1,0:T(8,128)S(1)} %get-tuple-element.50), channel_id=1, source_target_pairs={{8,0},{16,8},{24,16},{32,24},{40,32},{48,40},{56,48},{64,56},{72,6... | collective-permute-start | bytes 98312 | tf_op jit(solution)/shard_map/ppermute | solution.py:15
  15.9 20.6 %all-to-all-start = ((s32[32,1,32]{2,1,0:T(1,128)}), s32[32,1,32]{2,1,0:T(1,128)S(1)}, u32[]{:S(2)}, u32[]{:S(2)}) async-start(s32[32,1,32]{2,1,0:T(1,128)} %all_to_all.22), calls=%async_computation | async-start | bytes 32768 | tf_op jit(solution)/shard_map/all_to_all | solution.py:100
  27.3 27.3 %collective-permute-start.3 = (f32[1,32,256]{2,1,0:T(8,128)S(1)}, f32[1,32,256]{2,1,0:T(8,128)S(1)}, u32[]{:S(2)}, u32[]{:S(2)}) collective-permute-start(f32[1,32,256]{2,1,0:T(8,128)S(1)} %get-tuple-element.52), channel_id=1, source_target_pairs={{0,8},{8,16},{16,24},{24,32},{32,40},{40,48},{48,56},{56,64},{64,7... | collective-permute-start | bytes 98312 | tf_op jit(solution)/shard_map/ppermute | solution.py:14
  31.9 23.7 %collective-permute-start.1 = (f32[1,32,256]{2,1,0:T(8,128)S(1)}, f32[1,32,256]{2,1,0:T(8,128)S(1)}, u32[]{:S(2)}, u32[]{:S(2)}) collective-permute-start(f32[1,32,256]{2,1,0:T(8,128)S(1)} %get-tuple-element.51), channel_id=1, source_target_pairs={{8,0},{16,8},{24,16},{32,24},{40,32},{48,40},{56,48},{64,56},{72,6... | collective-permute-start | bytes 98312 | tf_op jit(solution)/shard_map/ppermute | solution.py:15
  36.6 27.8 %all-to-all-start.1 = ((bf16[32,32,128]{2,1,0:T(8,128)(2,1)}), bf16[32,32,128]{2,1,0:T(8,128)(2,1)S(1)}, u32[]{:S(2)}, u32[]{:S(2)}) async-start(bf16[32,32,128]{2,1,0:T(8,128)(2,1)} %bitcast.6), calls=%async_computation.1 | async-start | bytes 524288 | tf_op jit(solution)/shard_map/all_to_all | solution.py:93
  49.3 11.6 %collective-permute-start.4 = (f32[10,1,256]{2,1,0:T(1,128)S(1)}, f32[10,1,256]{2,1,0:T(1,128)S(1)}, u32[]{:S(2)}, u32[]{:S(2)}) collective-permute-start(f32[10,1,256]{2,1,0:T(1,128)S(1)} %get-tuple-element.32), channel_id=1, source_target_pairs={{1,0},{2,1},{3,2},{4,3},{5,4},{6,5},{7,6},{9,8},{10,9},{11,10},{12... | collective-permute-start | bytes 30728 | tf_op jit(solution)/shard_map/ppermute | solution.py:15
  50.6 10.3 %collective-permute-start.6 = (f32[10,1,256]{2,1,0:T(1,128)S(1)}, f32[10,1,256]{2,1,0:T(1,128)S(1)}, u32[]{:S(2)}, u32[]{:S(2)}) collective-permute-start(f32[10,1,256]{2,1,0:T(1,128)S(1)} %get-tuple-element.31), channel_id=1, source_target_pairs={{0,1},{1,2},{2,3},{3,4},{4,5},{5,6},{6,7},{8,9},{9,10},{10,11},{11... | collective-permute-start | bytes 30728 | tf_op jit(solution)/shard_map/ppermute | solution.py:14
  72.6 9.2 %collective-permute-start.9 = (f32[1,32,256]{2,1,0:T(8,128)S(1)}, f32[1,32,256]{2,1,0:T(8,128)S(1)}, u32[]{:S(2)}, u32[]{:S(2)}) collective-permute-start(f32[1,32,256]{2,1,0:T(8,128)S(1)} %slice.571), channel_id=1, source_target_pairs={{0,8},{8,16},{16,24},{24,32},{32,40},{40,48},{48,56},{56,64},{64,7... | collective-permute-start | bytes 98312 | tf_op jit(solution)/shard_map/ppermute | solution.py:14
  79.9 8.8 %collective-permute-start.8 = (f32[1,32,256]{2,1,0:T(8,128)S(1)}, f32[1,32,256]{2,1,0:T(8,128)S(1)}, u32[]{:S(2)}, u32[]{:S(2)}) collective-permute-start(f32[1,32,256]{2,1,0:T(8,128)S(1)} %slice.568), channel_id=1, source_target_pairs={{8,0},{16,8},{24,16},{32,24},{40,32},{48,40},{56,48},{64,56},{72,6... | collective-permute-start | bytes 98312 | tf_op jit(solution)/shard_map/ppermute | solution.py:15
  106.2 8.8 %collective-permute-start.12 = (f32[1,32,256]{2,1,0:T(8,128)S(1)}, f32[1,32,256]{2,1,0:T(8,128)S(1)}, u32[]{:S(2)}, u32[]{:S(2)}) collective-permute-start(f32[1,32,256]{2,1,0:T(8,128)S(1)} %slice.581), channel_id=1, source_target_pairs={{8,0},{16,8},{24,16},{32,24},{40,32},{48,40},{56,48},{64,56},{72,6... | collective-permute-start | bytes 98312 | tf_op jit(solution)/shard_map/ppermute | solution.py:15
  132.4 8.8 %collective-permute-start.16 = (f32[1,32,256]{2,1,0:T(8,128)S(1)}, f32[1,32,256]{2,1,0:T(8,128)S(1)}, u32[]{:S(2)}, u32[]{:S(2)}) collective-permute-start(f32[1,32,256]{2,1,0:T(8,128)S(1)} %slice.594), channel_id=1, source_target_pairs={{8,0},{16,8},{24,16},{32,24},{40,32},{48,40},{56,48},{64,56},{72,6... | collective-permute-start | bytes 98312 | tf_op jit(solution)/shard_map/ppermute | solution.py:15
  141.3 7.5 %collective-permute-start.18 = (f32[10,1,256]{2,1,0:T(1,128)S(1)}, f32[10,1,256]{2,1,0:T(1,128)S(1)}, u32[]{:S(2)}, u32[]{:S(2)}) collective-permute-start(f32[10,1,256]{2,1,0:T(1,128)S(1)} %get-tuple-element.26), channel_id=1, source_target_pairs={{1,0},{2,1},{3,2},{4,3},{5,4},{6,5},{7,6},{9,8},{10,9},{11,10},{12... | collective-permute-start | bytes 30728 | tf_op jit(solution)/shard_map/ppermute | solution.py:15
  160.3 8.8 %collective-permute-start.20 = (f32[1,32,256]{2,1,0:T(8,128)S(1)}, f32[1,32,256]{2,1,0:T(8,128)S(1)}, u32[]{:S(2)}, u32[]{:S(2)}) collective-permute-start(f32[1,32,256]{2,1,0:T(8,128)S(1)} %slice.607), channel_id=1, source_target_pairs={{8,0},{16,8},{24,16},{32,24},{40,32},{48,40},{56,48},{64,56},{72,6... | collective-permute-start | bytes 98312 | tf_op jit(solution)/shard_map/ppermute | solution.py:15
  169.1 8.0 %collective-permute-start.22 = (f32[10,1,256]{2,1,0:T(1,128)S(1)}, f32[10,1,256]{2,1,0:T(1,128)S(1)}, u32[]{:S(2)}, u32[]{:S(2)}) collective-permute-start(f32[10,1,256]{2,1,0:T(1,128)S(1)} %get-tuple-element.24), channel_id=1, source_target_pairs={{1,0},{2,1},{3,2},{4,3},{5,4},{6,5},{7,6},{9,8},{10,9},{11,10},{12... | collective-permute-start | bytes 30728 | tf_op jit(solution)/shard_map/ppermute | solution.py:15
  170.4 7.4 %collective-permute-start.23 = (f32[10,1,256]{2,1,0:T(1,128)S(1)}, f32[10,1,256]{2,1,0:T(1,128)S(1)}, u32[]{:S(2)}, u32[]{:S(2)}) collective-permute-start(f32[10,1,256]{2,1,0:T(1,128)S(1)} %get-tuple-element.23), channel_id=1, source_target_pairs={{0,1},{1,2},{2,3},{3,4},{4,5},{5,6},{6,7},{8,9},{9,10},{10,11},{11... | collective-permute-start | bytes 30728 | tf_op jit(solution)/shard_map/ppermute | solution.py:14
  188.7 8.8 %collective-permute-start.24 = (f32[1,32,256]{2,1,0:T(8,128)S(1)}, f32[1,32,256]{2,1,0:T(8,128)S(1)}, u32[]{:S(2)}, u32[]{:S(2)}) collective-permute-start(f32[1,32,256]{2,1,0:T(8,128)S(1)} %slice.620), channel_id=1, source_target_pairs={{8,0},{16,8},{24,16},{32,24},{40,32},{48,40},{56,48},{64,56},{72,6... | collective-permute-start | bytes 98312 | tf_op jit(solution)/shard_map/ppermute | solution.py:15
  197.5 8.0 %collective-permute-start.26 = (f32[10,1,256]{2,1,0:T(1,128)S(1)}, f32[10,1,256]{2,1,0:T(1,128)S(1)}, u32[]{:S(2)}, u32[]{:S(2)}) collective-permute-start(f32[10,1,256]{2,1,0:T(1,128)S(1)} %get-tuple-element.22), channel_id=1, source_target_pairs={{1,0},{2,1},{3,2},{4,3},{5,4},{6,5},{7,6},{9,8},{10,9},{11,10},{12... | collective-permute-start | bytes 30728 | tf_op jit(solution)/shard_map/ppermute | solution.py:15
  218.3 9.0 %collective-permute-start.28 = (f32[1,32,256]{2,1,0:T(8,128)}, f32[1,32,256]{2,1,0:T(8,128)S(1)}, u32[]{:S(2)}, u32[]{:S(2)}) collective-permute-start(f32[1,32,256]{2,1,0:T(8,128)} %slice.633), channel_id=1, source_target_pairs={{8,0},{16,8},{24,16},{32,24},{40,32},{48,40},{56,48},{64,56},{72,6... | collective-permute-start | bytes 98312 | tf_op jit(solution)/shard_map/ppermute | solution.py:15
  227.9 9.9 %collective-permute-start.30 = (f32[10,1,256]{2,1,0:T(1,128)}, f32[10,1,256]{2,1,0:T(1,128)S(1)}, u32[]{:S(2)}, u32[]{:S(2)}) collective-permute-start(f32[10,1,256]{2,1,0:T(1,128)} %get-tuple-element.20), channel_id=1, source_target_pairs={{1,0},{2,1},{3,2},{4,3},{5,4},{6,5},{7,6},{9,8},{10,9},{11,10},{12... | collective-permute-start | bytes 30728 | tf_op jit(solution)/shard_map/ppermute | solution.py:15
  229.2 8.6 %collective-permute-start.31 = (f32[10,1,256]{2,1,0:T(1,128)}, f32[10,1,256]{2,1,0:T(1,128)}, u32[]{:S(2)}, u32[]{:S(2)}) collective-permute-start(f32[10,1,256]{2,1,0:T(1,128)} %get-tuple-element.19), channel_id=1, source_target_pairs={{0,1},{1,2},{2,3},{3,4},{4,5},{5,6},{6,7},{8,9},{9,10},{10,11},{11... | collective-permute-start | bytes 30728 | tf_op jit(solution)/shard_map/ppermute | solution.py:14
  251.6 9.0 %collective-permute-start.32 = (f32[1,32,256]{2,1,0:T(8,128)}, f32[1,32,256]{2,1,0:T(8,128)S(1)}, u32[]{:S(2)}, u32[]{:S(2)}) collective-permute-start(f32[1,32,256]{2,1,0:T(8,128)} %slice.646), channel_id=1, source_target_pairs={{8,0},{16,8},{24,16},{32,24},{40,32},{48,40},{56,48},{64,56},{72,6... | collective-permute-start | bytes 98312 | tf_op jit(solution)/shard_map/ppermute | solution.py:15
  261.2 9.5 %collective-permute-start.34 = (f32[10,1,256]{2,1,0:T(1,128)}, f32[10,1,256]{2,1,0:T(1,128)S(1)}, u32[]{:S(2)}, u32[]{:S(2)}) collective-permute-start(f32[10,1,256]{2,1,0:T(1,128)} %get-tuple-element.18), channel_id=1, source_target_pairs={{1,0},{2,1},{3,2},{4,3},{5,4},{6,5},{7,6},{9,8},{10,9},{11,10},{12... | collective-permute-start | bytes 30728 | tf_op jit(solution)/shard_map/ppermute | solution.py:15
  262.5 8.2 %collective-permute-start.35 = (f32[10,1,256]{2,1,0:T(1,128)}, f32[10,1,256]{2,1,0:T(1,128)}, u32[]{:S(2)}, u32[]{:S(2)}) collective-permute-start(f32[10,1,256]{2,1,0:T(1,128)} %get-tuple-element.17), channel_id=1, source_target_pairs={{0,1},{1,2},{2,3},{3,4},{4,5},{5,6},{6,7},{8,9},{9,10},{10,11},{11... | collective-permute-start | bytes 30728 | tf_op jit(solution)/shard_map/ppermute | solution.py:14
  (16 other events, 204.8 us)
where the time goes:
time: 331 us; the launch traced here: 329 us
  starting transfers between devices  139 us (42%)
  other arithmetic  76.6 us (23%)
  waiting for transfers between devices  51.5 us (16%)
  local copies, waits for them, and re-layouts  41.1 us (12%)
  blocking collectives  19.1 us (6%)
    ppermute x18, starting transfers between devices, padded_2(): before = lax.ppermute(last, axis, up)  88.9 us
    scatter-add x8, other arithmetic, shards(): wave_next.reshape(-1).at[cell_ids].add(amplitudes[:, moment])  49.8 us
    ppermute x18, waiting for transfers between devices, padded_2(): after = lax.ppermute(leading, axis, down)  47.6 us
    ppermute x18, starting transfers between devices, padded_2(): after = lax.ppermute(leading, axis, down)  28.9 us
    all_to_all x1, blocking collectives, shards(): lax.all_to_all(coarse_block, 'gy', split_axis=1, concat_axis=2, tiled=True)  19.1 us
    reshape x1, local copies, waits for them, and re-layouts, coarsen(): blocks = kernel.reshape(size_a // 2, 2, size_b // 2, 2, size_c // 2, 2)  18.1 us
    all_to_all x1, starting transfers between devices, shards(): lax.all_to_all(codes.reshape(slab_count, slot_count), 'gx', split_axis=0,...  10.6 us
    all_to_all x1, starting transfers between devices, shards(): lax.all_to_all(packed.reshape(slab_count, slot_count, panel_len), 'gx', s...  10.3 us
  transfers between devices with their start and end apart: 38, of which 13 were waited for; matrix products, arithmetic and copies ran while one was open for 7% of the time, Pallas kernels for 0%

commit v1 on v0

v1 whole, which is shorter than its diff:
```python
import functools

import jax
import jax.numpy as jnp
from jax import lax
from jax.experimental import pallas as pl
from jax.experimental.pallas import tpu as pltpu
from jax.sharding import PartitionSpec as P

MESH = pl.DeviceIdType.MESH
F32, BF16, I32 = jnp.float32, jnp.bfloat16, jnp.int32


def dot_nt(a, b):
    return lax.dot_general(a, b, (((1,), (1,)), ((), ())), preferred_element_type=F32)


def iota(shape, dim):
    return lax.broadcasted_iota(I32, shape, dim)


def halves(value):
    high = value.astype(BF16)
    return high, (value - high.astype(F32)).astype(BF16)


def build_messages(res_ref, owner, cell, offset, msg_ref, table_ref):
    row, k = iota((256, 128), 0), iota((256, 128), 1)
    gap = jnp.abs(k + row // 8 - 16 * (row % 8 + 1))
    weights = jnp.maximum(16 - gap, 0).astype(F32).astype(BF16)
    table_ref[...] = dot_nt(weights, res_ref[...])
    amp = jnp.zeros((8, 512), F32)
    for shift in range(32):
        amp = amp + jnp.where(offset == shift, table_ref[8 * shift : 8 * shift + 8, :], 0.0)
    amp = amp * (1.0 / 64.0)
    member = (iota((32, 512), 0) == owner).astype(F32)
    earlier = (iota((512, 512), 0) < iota((512, 512), 1)).astype(F32).astype(BF16)
    counts = jnp.dot(member.astype(BF16), earlier, preferred_element_type=F32)
    rank = jnp.sum(member * counts, axis=0, keepdims=True)
    slot = owner * 32 + rank.astype(I32)
    high, low = halves(amp)
    which = iota((16, 512), 0)
    digits = jnp.where(which == 0, cell // 256, jnp.where(which == 1, cell % 256, 0))
    payload = jnp.concatenate(
        [high.astype(F32), low.astype(F32), digits.astype(F32)], axis=0
    ).astype(BF16)
    place = (iota((1024, 512), 0) == slot).astype(F32).astype(BF16)
    packed = dot_nt(payload, place)
    lane = iota((8, 128), 1)
    for o in range(32):
        block = slice(128 * (o // 4), 128 * (o // 4) + 128)
        amps = packed[0:8, block] + packed[8:16, block]
        cells = packed[16:24, block]
        back = 32 * (o % 4)
        if back:
            amps = pltpu.roll(amps, 128 - back, 1)
        ahead = (32 - back) % 128
        if ahead:
            cells = pltpu.roll(cells, ahead, 1)
        msg_ref[o] = jnp.where(lane < 32, amps, cells)


def collect(recv_ref, amp_ref, xy_ref, z_ref):
    lane = iota((8, 128), 1)
    xs, zs = [], []
    for g in range(8):
        amps = jnp.zeros((8, 128), F32)
        cells = jnp.zeros((8, 128), F32)
        for q in range(4):
            tile = recv_ref[4 * g + q]
            here = (lane // 32) == q
            moved = pltpu.roll(tile, 32 * q, 1) if q else tile
            amps = jnp.where(here, moved, amps)
            turn = (32 * q - 32) % 128
            moved = pltpu.roll(tile, turn, 1) if turn else tile
            cells = jnp.where(here, moved, cells)
        amp_ref[:, 128 * g : 128 * g + 128] = amps
        xs.append(cells[0:1, :])
        zs.append(cells[1:2, :])
    rows = iota((256, 1024), 0).astype(F32)
    xy_ref[...] = (rows == jnp.concatenate(xs, axis=1)).astype(F32).astype(BF16)
    z_ref[...] = (rows == jnp.concatenate(zs, axis=1)).astype(F32).astype(BF16)


def kernel(
    last_ref, now_ref, dens_ref, vel_ref, facc_hbm, res_ref, owner_ref, cell_ref, offset_ref,
    sens_ref, final_ref,
    wave, rho, ysend, yrecv, rsend, rrecv, coef, source, acc, facc, msg, recv, table,
    amp, xy, zz, usend, urecv,
    ss, rs, ds, dr, as_, ar, us, ur, fs,
):
    i, j = lax.axis_index("gx"), lax.axis_index("gy")
    nx, ny = 32, 8
    left, right = lax.rem(i + nx - 1, nx), lax.rem(i + 1, nx)
    lower, upper = lax.rem(j + ny - 1, ny), lax.rem(j + 1, ny)
    barrier = pltpu.get_barrier_semaphore()

    def greet_x(k, c):
        pl.semaphore_signal(
            barrier, inc=1, device_id=(lax.rem(i + k, nx), j), device_id_type=MESH
        )
        return c

    def greet_y(k, c):
        pl.semaphore_signal(
            barrier, inc=1, device_id=(i, lax.rem(j + k, ny)), device_id_type=MESH
        )
        return c

    lax.fori_loop(1, nx, greet_x, 0)
    lax.fori_loop(1, ny, greet_y, 0)
    forward = pltpu.make_async_copy(facc_hbm, facc, fs)
    forward.start()

    for x in range(8):
        ysend[0, 0, x : x + 1, :] = now_ref[x, 0:1, :]
        ysend[0, 1, x : x + 1, :] = now_ref[x, 31:32, :]
        rsend[0, x : x + 1, :] = dens_ref[x, 0:1, :]
        rsend[1, x : x + 1, :] = dens_ref[x, 31:32, :]
    wave[0, 1:9] = now_ref[...]
    wave[1, 1:9] = last_ref[...]
    rho[1:9] = dens_ref[...]
    build_messages(res_ref, owner_ref[...], cell_ref[...], offset_ref[...], msg, table)
    recv[i] = msg[i]
    acc[...] = jnp.zeros_like(acc)
    pl.semaphore_wait(barrier, nx + ny - 2)

    def remote(src, dst, send, receive, device):
        return pltpu.make_async_remote_copy(
            src_ref=src, dst_ref=dst, send_sem=send, recv_sem=receive,
            device_id=device, device_id_type=MESH,
        )

    def scatter(k):
        to = lax.rem(i + k, nx)
        return remote(msg.at[to], recv.at[i], as_.at[k], ar.at[k], (to, j))

    def begin(k, c):
        scatter(k).start()
        return c

    def end(k, c):
        scatter(k).wait()
        return c

    lax.fori_loop(1, nx, begin, 0)
    edges = [
        remote(dens_ref.at[0], rho.at[9], ds.at[0], dr.at[0], (left, j)),
        remote(dens_ref.at[7], rho.at[0], ds.at[1], dr.at[1], (right, j)),
        remote(rsend.at[0], rrecv.at[1], ds.at[2], dr.at[2], (i, lower)),
        remote(rsend.at[1], rrecv.at[0], ds.at[3], dr.at[3], (i, upper)),
        remote(now_ref.at[0], wave.at[0, 9], ss.at[0, 0], rs.at[0, 0], (left, j)),
        remote(now_ref.at[7], wave.at[0, 0], ss.at[0, 1], rs.at[0, 1], (right, j)),
    ]

    def halo_x(p):
        return [
            remote(wave.at[p, 1], wave.at[p, 9], ss.at[p, 0], rs.at[p, 0], (left, j)),
            remote(wave.at[p, 8], wave.at[p, 0], ss.at[p, 1], rs.at[p, 1], (right, j)),
        ]

    def halo_y(p):
        return [
            remote(ysend.at[p, 0], yrecv.at[p, 1], ss.at[p, 2], rs.at[p, 2], (i, lower)),
            remote(ysend.at[p, 1], yrecv.at[p, 0], ss.at[p, 3], rs.at[p, 3], (i, upper)),
        ]

    for copy in edges + halo_y(0):
        copy.start()
    for copy in edges[:4]:
        copy.wait()

    row, lane = iota((32, 256), 0), iota((32, 256), 1)
    has_low, has_high = (j > 0).astype(F32), (j < ny - 1).astype(F32)

    def couple(x, c):
        density = rho[x + 1]
        speed = 0.11 * vel_ref[x]
        stiff = speed * speed * density
        first = jnp.where(jnp.logical_and(x == 0, i == 0), 0.0, 1.0)
        final = jnp.where(jnp.logical_and(x == 7, i == nx - 1), 0.0, 1.0)
        low = rrecv[0, pl.ds(x, 1), :] * has_low
        high = rrecv[1, pl.ds(x, 1), :] * has_high
        near = [
            (rho[x + 2] * final, final),
            (rho[x] * first, first),
            (
                jnp.where(row == 31, high, pltpu.roll(density, 31, 0)),
                jnp.where(row == 31, has_high, 1.0),
            ),
            (
                jnp.where(row == 0, low, pltpu.roll(density, 1, 0)),
                jnp.where(row == 0, has_low, 1.0),
            ),
            (
                jnp.where(lane == 255, 0.0, pltpu.roll(density, 255, 1)),
                jnp.where(lane == 255, 0.0, 1.0),
            ),
            (
                jnp.where(lane == 0, 0.0, pltpu.roll(density, 1, 1)),
                jnp.where(lane == 0, 0.0, 1.0),
            ),
        ]
        centre = 2.0
        for n, (value, inside) in enumerate(near):
            strength = stiff * (2.0 / (density + value))
            centre = centre - strength
            coef[n + 1, x] = strength * inside
        coef[0, x] = centre
        return c

    lax.fori_loop(0, 8, couple, 0)
    lax.fori_loop(1, nx, end, 0)
    collect(recv, amp, xy, zz)

    def inject(t):
        high, low = halves(amp[pl.ds(t, 1), :])
        cells = xy[...]
        source[...] = (
            dot_nt(cells * high, zz[...]) + dot_nt(cells * low, zz[...])
        ).reshape(8, 32, 256)

    inject(0)
    forward.wait()

    def layer(t, p, x, out):
        w = wave[p, x + 1]
        up = jnp.where(row == 31, yrecv[p, 1, x : x + 1, :], pltpu.roll(w, 31, 0))
        down = jnp.where(row == 0, yrecv[p, 0, x : x + 1, :], pltpu.roll(w, 1, 0))
        value = coef[0, x] * w + (source[x] - wave[1 - p, x + 1])
        value = value + coef[1, x] * wave[p, x + 2] + coef[2, x] * wave[p, x]
        value = value + coef[3, x] * up + coef[4, x] * down
        value = value + coef[5, x] * pltpu.roll(w, 255, 1) + coef[6, x] * pltpu.roll(w, 1, 1)
        acc[x] += value * facc[t, x].astype(F32)
        if out:
            final_ref[x] = value
        else:
            wave[1 - p, x + 1] = value
            ysend[1 - p, 0, x : x + 1, :] = value[0:1, :]
            ysend[1 - p, 1, x : x + 1, :] = value[31:32, :]

    def step(t, c):
        p = lax.rem(t, 2)
        for copy in halo_x(p) + halo_y(p):
            copy.wait()
        for x in (0, 7):
            layer(t, p, x, False)
        for copy in halo_x(1 - p):
            copy.start()
        for x in range(1, 7):
            layer(t, p, x, False)
        for copy in halo_y(1 - p):
            copy.start()
        inject(t + 1)
        return c

    lax.fori_loop(0, 7, step, 0)
    for copy in halo_x(1) + halo_y(1):
        copy.wait()
    for x in range(8):
        layer(7, 1, x, True)

    pairs = []
    for a in range(4):
        both = (-2.0 / vel_ref[2 * a]) * acc[2 * a]
        pairs.append(both + (-2.0 / vel_ref[2 * a + 1]) * acc[2 * a + 1])
    high, low = halves(jnp.concatenate(pairs, axis=0))
    pool_y = (iota((128, 128), 0) == iota((128, 128), 1) // 2).astype(F32).astype(BF16)
    pool_z = (iota((128, 256), 0) == iota((128, 256), 1) // 2).astype(F32).astype(BF16)
    rows = jnp.dot(pool_y, high, preferred_element_type=F32) + jnp.dot(
        pool_y, low, preferred_element_type=F32
    )
    high, low = halves(rows)
    usend[...] = ((dot_nt(pool_z, high) + dot_nt(pool_z, low)) * 0.125).reshape(8, 16, 128)
    urecv[j] = usend[j]

    def spread(k):
        to = lax.rem(j + k, ny)
        return remote(usend.at[to], urecv.at[j], us.at[k], ur.at[k], (i, to))

    for k in range(1, ny):
        spread(k).start()
    for k in range(1, ny):
        spread(k).wait()
    strip = iota((16, 128), 1) // 16
    for a in range(4):
        total = jnp.zeros((16, 128), F32)
        for b in range(8):
            turn = (16 * b - 16 * a) % 128
            tile = urecv[b]
            moved = pltpu.roll(tile, turn, 1) if turn else tile
            total = jnp.where(strip == b, moved, total)
        sens_ref[a] = total


def shards(vel, dens, last, now, facc, res, owner, cell, offset):
    vm = pl.BlockSpec(memory_space=pltpu.VMEM)
    dma = pltpu.SemaphoreType.DMA
    sens, final = pl.pallas_call(
        kernel,
        name="adjoint",
        out_shape=(
            jax.ShapeDtypeStruct((4, 16, 128), F32),
            jax.ShapeDtypeStruct((8, 32, 256), F32),
        ),
        in_specs=[vm] * 4 + [pl.BlockSpec(memory_space=pl.ANY)] + [vm] * 4,
        out_specs=(vm, vm),
        scratch_shapes=[
            pltpu.VMEM((2, 10, 32, 256), F32),
            pltpu.VMEM((10, 32, 256), F32),
            pltpu.VMEM((2, 2, 8, 256), F32),
            pltpu.VMEM((2, 2, 8, 256), F32),
            pltpu.VMEM((2, 8, 256), F32),
            pltpu.VMEM((2, 8, 256), F32),
            pltpu.VMEM((7, 8, 32, 256), F32),
            pltpu.VMEM((8, 32, 256), F32),
            pltpu.VMEM((8, 32, 256), F32),
            pltpu.VMEM((8, 8, 32, 256), BF16),
            pltpu.VMEM((32, 8, 128), F32),
            pltpu.VMEM((32, 8, 128), F32),
            pltpu.VMEM((256, 512), F32),
            pltpu.VMEM((8, 1024), F32),
            pltpu.VMEM((256, 1024), BF16),
            pltpu.VMEM((256, 1024), BF16),
            pltpu.VMEM((8, 16, 128), F32),
            pltpu.VMEM((8, 16, 128), F32),
            dma((2, 4)), dma((2, 4)), dma((4,)), dma((4,)),
            dma((32,)), dma((32,)), dma((8,)), dma((8,)), dma(()),
        ],
        compiler_params=pltpu.CompilerParams(
            collective_id=0, has_side_effects=True, vmem_limit_bytes=48 << 20
        ),
    )(
        last, now, dens, vel, facc, res,
        owner.reshape(1, -1), cell.reshape(1, -1), offset.reshape(1, -1),
    )
    return sens, final


def solution(mesh):
    in_specs = (
        P("gx", "gy", None),
        P("gx", "gy", None),
        P("gx", "gy", None),
        P("gx", "gy", None),
        P(None, "gx", "gy", None),
        P(("gx", "gy"), None),
        P(("gx", "gy"), None),
        P(("gx", "gy")),
        P(("gx", "gy")),
    )
    out_specs = (P("gx", "gy", None), P("gx", "gy", None))
    return jax.shard_map(shards, mesh=mesh, in_specs=in_specs, out_specs=out_specs, check_vma=False)
```

time: 331 us -> 65.1 us (0.20)
  the two profiles are of different devices: /device:TPU:113 before, /device:TPU:8 now
where the time goes in v1:
time: 65.1 us; the launch traced here: 64.8 us
  Pallas kernels  55.5 us (85%)
  local copies, waits for them, and re-layouts  8.61 us (13%)
  between operations  0.67 us (1%)
    pallas_call x1, Pallas kernels, shards(): pl.pallas_call(kernel, name='adjoint', out_shape=(jax.ShapeDtypeStruct((4...  55.5 us
    unnamed x20, local copies, waits for them, and re-layouts  8.61 us

profile of v1, /device:TPU:8, one launch (start us, length us, event | category | flops | bytes accessed | tf_op | source)
XLA Modules:
  0.0 64.8 jit_solution(1898826608448328661)
XLA Ops:
  0.6 0.0 copy-start.7
  0.6 0.0 copy-start.6
  0.7 0.7 %copy-done.7 = s32[512]{0:T(512)S(1)} copy-done((s32[512]{0:T(512)S(1)}, s32[512]{0:T(512)}, u32[]{:S(2)}) %copy-start.7) | copy-done | bytes 2072
  1.3 0.0 copy-done.6
  1.3 0.0 copy-start
  1.3 1.2 %copy-done = bf16[8,8,32,256]{3,2,1,0:T(8,128)(2,1)S(1)} copy-done((bf16[8,8,32,256]{3,2,1,0:T(8,128)(2,1)S(1)}, bf16[8,8,32,256]{3,2,1,0:T(8,128)(2,1)}, u32[]{:S(2)}) %copy-start) | copy-done | bytes 1048600
  2.6 0.0 copy-start.1
  2.6 0.9 %copy-done.1 = f32[8,32,256]{2,1,0:T(8,128)S(1)} copy-done((f32[8,32,256]{2,1,0:T(8,128)S(1)}, f32[8,32,256]{2,1,0:T(8,128)}, u32[]{:S(2)}) %copy-start.1) | copy-done | bytes 262168
  3.5 0.0 copy-start.2
  3.5 0.9 %copy-done.2 = f32[8,32,256]{2,1,0:T(8,128)S(1)} copy-done((f32[8,32,256]{2,1,0:T(8,128)S(1)}, f32[8,32,256]{2,1,0:T(8,128)}, u32[]{:S(2)}) %copy-start.2) | copy-done | bytes 262168
  4.5 0.0 copy-start.3
  4.5 0.9 %copy-done.3 = f32[8,32,256]{2,1,0:T(8,128)S(1)} copy-done((f32[8,32,256]{2,1,0:T(8,128)S(1)}, f32[8,32,256]{2,1,0:T(8,128)}, u32[]{:S(2)}) %copy-start.3) | copy-done | bytes 262168
  5.4 0.0 copy-start.4
  5.4 0.9 %copy-done.4 = f32[8,32,256]{2,1,0:T(8,128)S(1)} copy-done((f32[8,32,256]{2,1,0:T(8,128)S(1)}, f32[8,32,256]{2,1,0:T(8,128)}, u32[]{:S(2)}) %copy-start.4) | copy-done | bytes 262168
  6.4 0.0 copy-start.5
  6.4 0.9 %copy-done.5 = bf16[512,128]{1,0:T(8,128)(2,1)S(1)} copy-done((bf16[512,128]{1,0:T(8,128)(2,1)S(1)}, bf16[512,128]{1,0:T(8,128)(2,1)}, u32[]{:S(2)}) %copy-start.5) | copy-done | bytes 131096
  7.3 0.0 copy-start.8
  7.3 0.7 %copy-done.8 = s32[512]{0:T(512)S(1)} copy-done((s32[512]{0:T(512)S(1)}, s32[512]{0:T(512)}, u32[]{:S(2)}) %copy-start.8) | copy-done | bytes 2072
  7.9 55.5 %adjoint.1 = (f32[4,16,128]{2,1,0:T(8,128)S(1)}, f32[8,32,256]{2,1,0:T(8,128)S(1)}) custom-call(f32[8,32,256]{2,1,0:T(8,128)S(1)} %copy-done.1, f32[8,32,256]{2,1,0:T(8,128)S(1)} %copy-done.2, f32[8,32,256]{2,1,0:T(8,128)S(1)} %copy-done.3, f32[8,32,256]{2,1,0:T(8,128)S(1)} %copy-done.4, bf16[8,8,32,256]{3,2,1,0:T(8,128)(2,1)S(1)} %copy-done, ...), custom_call_target="tpu_custom_call" | custom-call | tf_op jit(solution)/shard_map/adjoint/pallas_call | solution.py:299
  63.5 0.6 copy.13
  64.1 0.7 %copy.14 = f32[8,32,256]{2,1,0:T(8,128)} copy(f32[8,32,256]{2,1,0:T(8,128)S(1)} %get-tuple-element.5) | data formatting | bytes 524288
Async XLA Ops:
  0.6 0.7 %copy-start.7 = (s32[512]{0:T(512)S(1)}, s32[512]{0:T(512)}, u32[]{:S(2)}) copy-start(s32[512]{0:T(512)} %param.16) | copy-start | bytes 6148
  0.6 0.7 %copy-start.6 = (s32[512,1]{0,1:T(1,128)S(1)}, s32[512,1]{0,1:T(1,128)}, u32[]{:S(2)}) copy-start(s32[512,1]{0,1:T(1,128)} %param.15) | copy-start | bytes 6148
  1.3 1.2 %copy-start = (bf16[8,8,32,256]{3,2,1,0:T(8,128)(2,1)S(1)}, bf16[8,8,32,256]{3,2,1,0:T(8,128)(2,1)}, u32[]{:S(2)}) copy-start(bf16[8,8,32,256]{3,2,1,0:T(8,128)(2,1)} %facc_hbm.1) | copy-start | bytes 3145732
  2.6 0.9 %copy-start.1 = (f32[8,32,256]{2,1,0:T(8,128)S(1)}, f32[8,32,256]{2,1,0:T(8,128)}, u32[]{:S(2)}) copy-start(f32[8,32,256]{2,1,0:T(8,128)} %last_ref.1) | copy-start | bytes 786436
  3.5 0.9 %copy-start.2 = (f32[8,32,256]{2,1,0:T(8,128)S(1)}, f32[8,32,256]{2,1,0:T(8,128)}, u32[]{:S(2)}) copy-start(f32[8,32,256]{2,1,0:T(8,128)} %now_ref.1) | copy-start | bytes 786436
  4.5 0.9 %copy-start.3 = (f32[8,32,256]{2,1,0:T(8,128)S(1)}, f32[8,32,256]{2,1,0:T(8,128)}, u32[]{:S(2)}) copy-start(f32[8,32,256]{2,1,0:T(8,128)} %dens_ref.1) | copy-start | bytes 786436
  5.4 0.9 %copy-start.4 = (f32[8,32,256]{2,1,0:T(8,128)S(1)}, f32[8,32,256]{2,1,0:T(8,128)}, u32[]{:S(2)}) copy-start(f32[8,32,256]{2,1,0:T(8,128)} %vel_ref.1) | copy-start | bytes 786436
  6.4 0.9 %copy-start.5 = (bf16[512,128]{1,0:T(8,128)(2,1)S(1)}, bf16[512,128]{1,0:T(8,128)(2,1)}, u32[]{:S(2)}) copy-start(bf16[512,128]{1,0:T(8,128)(2,1)} %res_ref.1) | copy-start | bytes 393220
  7.3 0.7 %copy-start.8 = (s32[512]{0:T(512)S(1)}, s32[512]{0:T(512)}, u32[]{:S(2)}) copy-start(s32[512]{0:T(512)} %param.17) | copy-start | bytes 6148

commit v2 on v1

v2 whole, which is shorter than its diff:
```python
import functools

import jax
import jax.numpy as jnp
from jax import lax
from jax.experimental import pallas as pl
from jax.experimental.pallas import tpu as pltpu
from jax.sharding import PartitionSpec as P

MESH = pl.DeviceIdType.MESH
F32, BF16, I32 = jnp.float32, jnp.bfloat16, jnp.int32


def dot_nt(a, b):
    return lax.dot_general(a, b, (((1,), (1,)), ((), ())), preferred_element_type=F32)


def iota(shape, dim):
    return lax.broadcasted_iota(I32, shape, dim)


def halves(value):
    high = value.astype(BF16)
    return high, (value - high.astype(F32)).astype(BF16)


def build_messages(res_ref, owner, cell, offset, msg_ref, table_ref):
    row, k = iota((256, 128), 0), iota((256, 128), 1)
    gap = jnp.abs(k + row // 8 - 16 * (row % 8 + 1))
    weights = jnp.maximum(16 - gap, 0).astype(F32).astype(BF16)
    table_ref[...] = dot_nt(weights, res_ref[...])
    amp = jnp.zeros((8, 512), F32)
    for shift in range(32):
        amp = amp + jnp.where(offset == shift, table_ref[8 * shift : 8 * shift + 8, :], 0.0)
    amp = amp * (1.0 / 64.0)
    member = (iota((32, 512), 0) == owner).astype(F32)
    earlier = (iota((512, 512), 0) < iota((512, 512), 1)).astype(F32).astype(BF16)
    counts = jnp.dot(member.astype(BF16), earlier, preferred_element_type=F32)
    rank = jnp.sum(member * counts, axis=0, keepdims=True)
    slot = owner * 32 + rank.astype(I32)
    high, low = halves(amp)
    which = iota((16, 512), 0)
    digits = jnp.where(which == 0, cell // 256, jnp.where(which == 1, cell % 256, 0))
    payload = jnp.concatenate(
        [high.astype(F32), low.astype(F32), digits.astype(F32)], axis=0
    ).astype(BF16)
    place = (iota((1024, 512), 0) == slot).astype(F32).astype(BF16)
    packed = dot_nt(payload, place)
    lane = iota((8, 128), 1)
    for o in range(32):
        block = slice(128 * (o // 4), 128 * (o // 4) + 128)
        amps = packed[0:8, block] + packed[8:16, block]
        cells = packed[16:24, block]
        back = 32 * (o % 4)
        if back:
            amps = pltpu.roll(amps, 128 - back, 1)
        ahead = (32 - back) % 128
        if ahead:
            cells = pltpu.roll(cells, ahead, 1)
        msg_ref[o] = jnp.where(lane < 32, amps, cells)


def collect(recv_ref, amp_ref, xy_ref, z_ref):
    lane = iota((8, 128), 1)
    xs, zs = [], []
    for g in range(8):
        amps = jnp.zeros((8, 128), F32)
        cells = jnp.zeros((8, 128), F32)
        for q in range(4):
            tile = recv_ref[4 * g + q]
            here = (lane // 32) == q
            moved = pltpu.roll(tile, 32 * q, 1) if q else tile
            amps = jnp.where(here, moved, amps)
            turn = (32 * q - 32) % 128
            moved = pltpu.roll(tile, turn, 1) if turn else tile
            cells = jnp.where(here, moved, cells)
        amp_ref[:, 128 * g : 128 * g + 128] = amps
        xs.append(cells[0:1, :])
        zs.append(cells[1:2, :])
    rows = iota((256, 1024), 0).astype(F32)
    xy_ref[...] = (rows == jnp.concatenate(xs, axis=1)).astype(F32).astype(BF16)
    z_ref[...] = (rows == jnp.concatenate(zs, axis=1)).astype(F32).astype(BF16)


def couplings(density, speed, near):
    lane = iota(density.shape, density.ndim - 1)
    near = near + [
        (
            jnp.where(lane == 255, 0.0, pltpu.roll(density, 255, 1)),
            jnp.where(lane == 255, 0.0, 1.0),
        ),
        (jnp.where(lane == 0, 0.0, pltpu.roll(density, 1, 1)), jnp.where(lane == 0, 0.0, 1.0)),
    ]
    speed = 0.11 * speed
    stiff = speed * speed * density
    centre, weights = 2.0, []
    for value, inside in near:
        strength = stiff * (2.0 / (density + value))
        centre = centre - strength
        weights.append(strength * inside)
    return [centre] + weights


def advance(weight, w, xp, xm, yp, ym, prev, injected):
    value = weight(0) * w + (injected - prev)
    value = value + weight(1) * xp + weight(2) * xm
    value = value + weight(3) * yp + weight(4) * ym
    return value + weight(5) * pltpu.roll(w, 255, 1) + weight(6) * pltpu.roll(w, 1, 1)


def shifted(w, above, below):
    n = w.shape[0]
    row = iota(w.shape, 0)
    up = jnp.where(row == n - 1, above, pltpu.roll(w, n - 1, 0))
    down = jnp.where(row == 0, below, pltpu.roll(w, 1, 0))
    return up, down


def kernel(
    last_hbm, now_hbm, dens_hbm, vel_hbm, facc_hbm, res_hbm, owner_hbm, cell_hbm, offset_hbm,
    sens_ref, final_ref,
    vel, res_ref, owner_ref, cell_ref, offset_ref, rho, wave, acc, facc,
    coef, coefx, coefy, src_e, src_o,
    hx, hodd, yodd, ysend, yrecv, csend, crecv,
    sxr, sysend, syr, rhx, vhx, stsend, strecv, rcsend, rcrecv,
    msg, recv, table, amp, xy, zz, usend, urecv,
    xs, xr, es, er, gs, gr, cs, cr, as_, ar, us, ur, fs,
):
    i, j = lax.axis_index("gx"), lax.axis_index("gy")
    nx, ny = 32, 8
    xside = (lax.rem(i + nx - 1, nx), lax.rem(i + 1, nx))
    yside = (lax.rem(j + ny - 1, ny), lax.rem(j + 1, ny))
    barrier = pltpu.get_barrier_semaphore()

    loads = [
        pltpu.make_async_copy(src, dst, fs.at[n])
        for n, (src, dst) in enumerate(
            [
                (res_hbm, res_ref), (offset_hbm, offset_ref), (owner_hbm, owner_ref),
                (cell_hbm, cell_ref), (now_hbm, wave.at[0]), (dens_hbm, rho), (vel_hbm, vel),
                (last_hbm, wave.at[1]), (facc_hbm, facc),
            ]
        )
    ]
    for copy in loads:
        copy.start()

    def greet(device):
        pl.semaphore_signal(barrier, inc=1, device_id=device, device_id_type=MESH)

    def greet_x(k, c):
        greet((lax.rem(i + k, nx), j))
        return c

    def greet_y(k, c):
        greet((i, lax.rem(j + k, ny)))
        return c

    lax.fori_loop(1, nx, greet_x, 0)
    lax.fori_loop(1, ny, greet_y, 0)
    for a in range(2):
        for b in range(2):
            greet((xside[a], yside[b]))
    for copy in loads[:4]:
        copy.wait()
    build_messages(res_ref, owner_ref[...], cell_ref[...], offset_ref[...], msg, table)
    recv[i] = msg[i]
    for copy in loads[4:8]:
        copy.wait()

    def keep_rows(x, value):
        ysend[0, 0, x : x + 1, :] = value[0:1, :]
        ysend[0, 1, x : x + 1, :] = value[1:2, :]
        ysend[1, 0, x : x + 1, :] = value[31:32, :]
        ysend[1, 1, x : x + 1, :] = value[30:31, :]

    def keep_corners(dst, a, value):
        dst[2 * a] = value[0:1, :]
        dst[2 * a + 1] = value[31:32, :]

    for x in range(8):
        keep_rows(x, wave[0, x])
        for side, rows in enumerate(((0, 1), (31, 30))):
            near, far = rows
            stsend[side, 0, x : x + 1, :] = rho[x, near : near + 1, :]
            stsend[side, 1, x : x + 1, :] = rho[x, far : far + 1, :]
            stsend[side, 2, x : x + 1, :] = vel[x, near : near + 1, :]
            stsend[side, 3, x : x + 1, :] = wave[1, x, near : near + 1, :]
    for a in range(2):
        keep_corners(csend, a, wave[0, 7 * a])
        keep_corners(rcsend, a, rho[7 * a])
    pl.semaphore_wait(barrier, nx + ny + 2)

    def remote(src, dst, send, receive, device):
        return pltpu.make_async_remote_copy(
            src_ref=src, dst_ref=dst, send_sem=send, recv_sem=receive,
            device_id=device, device_id_type=MESH,
        )

    def scatter(k):
        to = lax.rem(i + k, nx)
        return remote(msg.at[to], recv.at[i], as_.at[k], ar.at[k], (to, j))

    def begin(k, c):
        scatter(k).start()
        return c

    def end(k, c):
        scatter(k).wait()
        return c

    lax.fori_loop(1, nx, begin, 0)

    def move_x(p):
        return [
            remote(wave.at[0, pl.ds(6 * a, 2)], hx.at[p, 1 - a], xs.at[p, a], xr.at[p, a],
                   (xside[a], j))
            for a in range(2)
        ]

    def move_y(p):
        return [
            remote(ysend.at[b], yrecv.at[p, 1 - b], xs.at[p, 2 + b], xr.at[p, 2 + b],
                   (i, yside[b]))
            for b in range(2)
        ]

    def move_c(p):
        return [
            remote(csend.at[2 * a + b], crecv.at[p, 3 - 2 * a - b], cs.at[p, 2 * a + b],
                   cr.at[p, 2 * a + b], (xside[a], yside[b]))
            for a in range(2) for b in range(2)
        ]

    def move_s(p):
        return [
            remote(src_e.at[7 * a], sxr.at[p, 1 - a], gs.at[p, a], gr.at[p, a], (xside[a], j))
            for a in range(2)
        ] + [
            remote(sysend.at[b], syr.at[p, 1 - b], gs.at[p, 2 + b], gr.at[p, 2 + b],
                   (i, yside[b]))
            for b in range(2)
        ]

    statics = []
    for a in range(2):
        statics += [
            (rho.at[pl.ds(6 * a, 2)], rhx.at[1 - a], (xside[a], j)),
            (vel.at[7 * a], vhx.at[1 - a], (xside[a], j)),
            (wave.at[1, 7 * a], hodd.at[1 - a], (xside[a], j)),
            (stsend.at[a], strecv.at[1 - a], (i, yside[a])),
        ]
        for b in range(2):
            n = 2 * a + b
            statics.append((rcsend.at[n], rcrecv.at[3 - n], (xside[a], yside[b])))
    statics = [
        remote(src, dst, es.at[n], er.at[n], to) for n, (src, dst, to) in enumerate(statics)
    ]
    for copy in statics + move_c(0) + move_x(0) + move_y(0):
        copy.start()
    acc[...] = jnp.zeros_like(acc)
    for copy in loads[8:] + statics:
        copy.wait()
    yodd[...] = strecv[:, 3]

    row = iota((32, 256), 0)
    row8 = iota((8, 256), 0)
    has_low, has_high = (j > 0).astype(F32), (j < ny - 1).astype(F32)
    has_left, has_right = (i > 0).astype(F32), (i < nx - 1).astype(F32)

    def along_y(density, above, below):
        up, down = shifted(density, above * has_high, below * has_low)
        return [
            (up, jnp.where(row == 31, has_high, 1.0)),
            (down, jnp.where(row == 0, has_low, 1.0)),
        ]

    def couple(x, xp, xm, first, final):
        density = rho[x]
        near = [(xp * final, final), (xm * first, first)]
        near += along_y(density, strecv[1, 0, pl.ds(x, 1), :], strecv[0, 0, pl.ds(x, 1), :])
        for n, value in enumerate(couplings(density, vel[x], near)):
            coef[n, x] = value

    def couple_inner(x, c):
        couple(x, rho[x + 1], rho[x - 1], 1.0, 1.0)
        return c

    couple(0, rho[1], rhx[0, 1], has_left, 1.0)
    couple(7, rhx[1, 0], rho[6], 1.0, has_right)
    lax.fori_loop(1, 7, couple_inner, 0)
    for a in range(2):
        density = rhx[a, 1 - a]
        outer, inner = rhx[a, a], rho[7 * a]
        xp, xm = (outer, inner) if a else (inner, outer)
        near = [(xp, 1.0), (xm, 1.0)] + along_y(density, rcrecv[2 * a + 1], rcrecv[2 * a])
        for n, value in enumerate(couplings(density, vhx[a], near)):
            coefx[a, n] = value
    for b in range(2):
        density = strecv[b, 0]
        outer, inner = strecv[b, 1], stsend[b, 0]
        yp, ym = (outer, inner) if b else (inner, outer)
        xp, xm = shifted(density, rcrecv[2 + b] * has_right, rcrecv[b] * has_left)
        near = [
            (xp, jnp.where(row8 == 7, has_right, 1.0)),
            (xm, jnp.where(row8 == 0, has_left, 1.0)),
            (yp, 1.0),
            (ym, 1.0),
        ]
        for n, value in enumerate(couplings(density, strecv[b, 2], near)):
            coefy[b, n] = value

    lax.fori_loop(1, nx, end, 0)
    collect(recv, amp, xy, zz)

    def inject(t, dst):
        high, low = halves(amp[pl.ds(t, 1), :])
        cells = xy[...]
        dst[...] = (dot_nt(cells * high, zz[...]) + dot_nt(cells * low, zz[...])).reshape(
            8, 32, 256
        )

    def prepare(t, p):
        inject(t, src_e)
        for x in range(8):
            sysend[0, x : x + 1, :] = src_e[x, 0:1, :]
            sysend[1, x : x + 1, :] = src_e[x, 31:32, :]
        for copy in move_s(p):
            copy.start()
        inject(t + 1, src_o)

    prepare(0, 0)

    def even_layer(t, p, x):
        w = wave[0, x]
        yp, ym = shifted(w, yrecv[p, 1, 0, x : x + 1, :], yrecv[p, 0, 0, x : x + 1, :])
        xp = wave[0, x + 1] if x < 7 else hx[p, 1, 0]
        xm = wave[0, x - 1] if x > 0 else hx[p, 0, 1]
        value = advance(lambda n: coef[n, x], w, xp, xm, yp, ym, wave[1, x], src_e[x])
        acc[x] += value * facc[t, x].astype(F32)
        wave[1, x] = value

    def odd_layer(t, x, out):
        w = wave[1, x]
        yp, ym = shifted(w, yodd[1, x : x + 1, :], yodd[0, x : x + 1, :])
        xp = wave[1, x + 1] if x < 7 else hodd[1]
        xm = wave[1, x - 1] if x > 0 else hodd[0]
        value = advance(lambda n: coef[n, x], w, xp, xm, yp, ym, wave[0, x], src_o[x])
        acc[x] += value * facc[t, x].astype(F32)
        if out:
            final_ref[x] = value
        else:
            wave[0, x] = value
            keep_rows(x, value)
            if x in (0, 7):
                keep_corners(csend, x // 7, value)

    def halo_layers(p):
        for a in range(2):
            w = hx[p, a, 1 - a]
            outer, inner = hx[p, a, a], wave[0, 7 * a]
            xp, xm = (outer, inner) if a else (inner, outer)
            yp, ym = shifted(w, crecv[p, 2 * a + 1], crecv[p, 2 * a])
            hodd[a] = advance(lambda n: coefx[a, n], w, xp, xm, yp, ym, hodd[a], sxr[p, a])
        for b in range(2):
            w = yrecv[p, b, 0]
            outer, inner = yrecv[p, b, 1], ysend[b, 0]
            yp, ym = (outer, inner) if b else (inner, outer)
            xp, xm = shifted(w, crecv[p, 2 + b], crecv[p, b])
            yodd[b] = advance(lambda n: coefy[b, n], w, xp, xm, yp, ym, yodd[b], syr[p, b])

    def pair(r, p, final):
        for copy in move_x(p) + move_y(p):
            copy.wait()
        for x in range(8):
            even_layer(2 * r, p, x)
        for copy in move_c(p) + move_s(p):
            copy.wait()
        halo_layers(p)
        if final:
            for x in range(8):
                odd_layer(2 * r + 1, x, True)
            return
        for x in (0, 7, 1, 6):
            odd_layer(2 * r + 1, x, False)
        for copy in move_c(1 - p) + move_x(1 - p):
            copy.start()
        for x in range(2, 6):
            odd_layer(2 * r + 1, x, False)
        for copy in move_y(1 - p):
            copy.start()
        prepare(2 * r + 2, 1 - p)

    def pair_step(r, c):
        pair(r, lax.rem(r, 2), False)
        return c

    lax.fori_loop(0, 3, pair_step, 0)
    pair(3, 1, True)

    pairs = []
    for a in range(4):
        both = (-2.0 / vel[2 * a]) * acc[2 * a]
        pairs.append(both + (-2.0 / vel[2 * a + 1]) * acc[2 * a + 1])
    high, low = halves(jnp.concatenate(pairs, axis=0))
    pool_y = (iota((128, 128), 0) == iota((128, 128), 1) // 2).astype(F32).astype(BF16)
    pool_z = (iota((128, 256), 0) == iota((128, 256), 1) // 2).astype(F32).astype(BF16)
    rows = jnp.dot(pool_y, high, preferred_element_type=F32) + jnp.dot(
        pool_y, low, preferred_element_type=F32
    )
    high, low = halves(rows)
    usend[...] = ((dot_nt(pool_z, high) + dot_nt(pool_z, low)) * 0.125).reshape(8, 16, 128)
    urecv[j] = usend[j]

    def spread(k):
        to = lax.rem(j + k, ny)
        return remote(usend.at[to], urecv.at[j], us.at[k], ur.at[k], (i, to))

    for k in range(1, ny):
        spread(k).start()
    for k in range(1, ny):
        spread(k).wait()
    strip = iota((16, 128), 1) // 16
    for a in range(4):
        total = jnp.zeros((16, 128), F32)
        for b in range(8):
            turn = (16 * b - 16 * a) % 128
            tile = urecv[b]
            moved = pltpu.roll(tile, turn, 1) if turn else tile
            total = jnp.where(strip == b, moved, total)
        sens_ref[a] = total


def shards(vel, dens, last, now, facc, res, owner, cell, offset):
    vm = pl.BlockSpec(memory_space=pltpu.VMEM)
    dma = pltpu.SemaphoreType.DMA
    field, plane, line = (8, 32, 256), (32, 256), (8, 256)
    f32 = lambda *shape: pltpu.VMEM(shape, F32)
    sens, final = pl.pallas_call(
        kernel,
        name="adjoint",
        out_shape=(
            jax.ShapeDtypeStruct((4, 16, 128), F32),
            jax.ShapeDtypeStruct(field, F32),
        ),
        in_specs=[pl.BlockSpec(memory_space=pltpu.HBM)] * 9,
        out_specs=(vm, vm),
        scratch_shapes=[
            f32(*field), pltpu.VMEM((512, 128), BF16), pltpu.VMEM((1, 512), I32),
            pltpu.VMEM((1, 512), I32), pltpu.VMEM((1, 512), I32),
            f32(*field), f32(2, *field), f32(*field), pltpu.VMEM((8, *field), BF16),
            f32(7, *field), f32(2, 7, *plane), f32(2, 7, *line), f32(*field), f32(*field),
            f32(2, 2, 2, *plane), f32(2, *plane), f32(2, *line), f32(2, 2, *line),
            f32(2, 2, 2, *line), f32(4, 1, 256), f32(2, 4, 1, 256),
            f32(2, 2, *plane), f32(2, *line), f32(2, 2, *line),
            f32(2, 2, *plane), f32(2, *plane), f32(2, 4, *line), f32(2, 4, *line),
            f32(4, 1, 256), f32(4, 1, 256),
            f32(32, 8, 128), f32(32, 8, 128), f32(256, 512), f32(8, 1024),
            pltpu.VMEM((256, 1024), BF16), pltpu.VMEM((256, 1024), BF16),
            f32(8, 16, 128), f32(8, 16, 128),
            dma((2, 4)), dma((2, 4)), dma((12,)), dma((12,)), dma((2, 4)), dma((2, 4)),
            dma((2, 4)), dma((2, 4)), dma((32,)), dma((32,)), dma((8,)), dma((8,)), dma((9,)),
        ],
        compiler_params=pltpu.CompilerParams(
            collective_id=0, has_side_effects=True, vmem_limit_bytes=67043328
        ),
    )(
        last, now, dens, vel, facc, res,
        owner.reshape(1, -1), cell.reshape(1, -1), offset.reshape(1, -1),
    )
    return sens, final


def solution(mesh):
    in_specs = (
        P("gx", "gy", None),
        P("gx", "gy", None),
        P("gx", "gy", None),
        P("gx", "gy", None),
        P(None, "gx", "gy", None),
        P(("gx", "gy"), None),
        P(("gx", "gy"), None),
        P(("gx", "gy")),
        P(("gx", "gy")),
    )
    out_specs = (P("gx", "gy", None), P("gx", "gy", None))
    return jax.shard_map(shards, mesh=mesh, in_specs=in_specs, out_specs=out_specs, check_vma=False)
```

time: 65.1 us -> 52.6 us (0.81)
  the two profiles are of different devices: /device:TPU:8 before, /device:TPU:1 now
where the time goes in v2:
time: 52.6 us; the launch traced here: 52.4 us
  Pallas kernels  48.7 us (93%)
  local copies, waits for them, and re-layouts  3.05 us (6%)
  between operations  0.64 us (1%)
    pallas_call x1, Pallas kernels, shards(): pl.pallas_call(kernel, name='adjoint', out_shape=(jax.ShapeDtypeStruct((4...  48.7 us
    unnamed x2, local copies, waits for them, and re-layouts  3.05 us

profile of v2, /device:TPU:1, one launch (start us, length us, event | category | flops | bytes accessed | tf_op | source)
XLA Modules:
  0.0 52.4 jit_solution(16611041843646007878)
XLA Ops:
  0.6 48.7 %adjoint.1 = (f32[4,16,128]{2,1,0:T(8,128)}, f32[8,32,256]{2,1,0:T(8,128)}) custom-call(f32[8,32,256]{2,1,0:T(8,128)} %last_hbm.1, f32[8,32,256]{2,1,0:T(8,128)} %now_hbm.1, f32[8,32,256]{2,1,0:T(8,128)} %dens_hbm.1, f32[8,32,256]{2,1,0:T(8,128)} %vel_hbm.1, bf16[8,8,32,256]{3,2,1,0:T(8,128)(2,1)} %facc_hbm.1, bf16[512,128]{1,0:T(8,128)(2,1)} %res_hbm.1, ...), custom_call_target="tpu_custom_call" | custom-call | tf_op jit(solution)/shard_map/adjoint/pallas_call | solution.py:439
  49.4 1.4 %copy.13 = f32[4,16,128]{2,1,0:T(8,128)} copy(f32[4,16,128]{2,1,0:T(8,128)} %get-tuple-element.4) | data formatting | bytes 65536
  50.7 1.7 %copy.14 = f32[8,32,256]{2,1,0:T(8,128)} copy(f32[8,32,256]{2,1,0:T(8,128)} %get-tuple-element.5) | data formatting | bytes 524288
